TPU v7x, 256 devices: a whole 4x4x8 slice. The times are simulated.
256 devices in a mesh: facet: 16 (over z, core), row: 8 (over x_hi, y), sub: 2 (over x_lo).
Axes of the slice: x: 4 (x_hi: 2, x_lo: 2; x = x_hi * 2 + x_lo), y: 4, z: 8, core: 2. Of those that a mesh axis runs over, the one named last changes fastest.
Arguments:
- facet_model: bfloat16 [2, 4, 8192, 8192], P(None, 'sub', ('facet', 'row')), may hold values from -6 to 6
- sub_offsets: int32 [256], replicated, may hold values from 0 to 65535
- tile_rows: int32 [256, 4], P(('facet', 'row', 'sub')), may hold values from 0 to 120
- tile_counts: int32 [256], P(('facet', 'row', 'sub')), may hold values from 1 to 4, as said below
- visibilities: bfloat16 [256, 4, 32, 8, 256], P(('facet', 'row', 'sub')), may hold values from -6 to 6
Outputs:
- residual_facets: bfloat16 [2, 4, 8192, 8192], P(None, 'sub', ('facet', 'row'))
- residual_vis: bfloat16 [256, 4, 32, 8, 256], P(('facet', 'row', 'sub'))
Inputs may be any that keep to these rules, and one draw needn't show every extreme that they name: tile_counts[s] tiles of subgrid s are live, the first ones; some subgrid has all 4 tiles live. Tile j of subgrid s covers subgrid rows tile_rows[s, j] to tile_rows[s, j] + 7; tiles may intersect.
All inputs are finite; a program needn't handle non-finite values.
Results may differ from a plain program's by a relative error of at most 0.014.
Values may be sent and summed in bfloat16 or wider, within the bound.
No kernel may reach another device: no remote copies, remote signals or barrier semaphores. Data moves between devices by JAX's collectives and lax.ppermute only.
A program may use at most 128 MiB of HBM per device.

v0:
```python
import math
import jax
import jax.numpy as jnp
from jax import lax
from jax.sharding import PartitionSpec as P

SKY = 65536
CS = 64
SG = 128
two_pi = 2.0 * math.pi


def modmul(left, right, modulus):
    lower = right % 256
    upper = right // 256
    return (left * lower % modulus + left * upper % modulus * 256) % modulus


def window_taper(pixels):
    places = jnp.arange(pixels, dtype=jnp.float32)
    curve = jnp.sin(math.pi * (places + 0.5) / pixels)
    return 0.25 + 0.75 * curve * curve


def turn_pair(phase_index, modulus):
    angle = phase_index.astype(jnp.float32) * (-two_pi / modulus)
    return (jnp.cos(angle), jnp.sin(angle))


def column_table(facet_ids, pixels, width, modulus, ratio):
    spacing = modulus // pixels
    column_pos = facet_ids // ratio % ratio * pixels
    freqs = spacing * jnp.arange(width, dtype=jnp.int32)
    places = (column_pos[:, None] + jnp.arange(pixels, dtype=jnp.int32)[None, :]) % modulus
    cosine, sine = turn_pair(modmul(freqs[None, :, None], places[:, None, :], modulus), modulus)
    scaled = window_taper(pixels) / math.sqrt(pixels)
    return (jnp.stack([cosine, sine], axis=1) * scaled).astype(jnp.bfloat16)


def row_block(offsets, pixels, width, modulus, count):
    spacing = modulus // pixels
    freqs = (offsets[:, None] + spacing * jnp.arange(width, dtype=jnp.int32)[None, :]) % modulus
    places = jnp.arange(count, dtype=jnp.int32)
    cosine, sine = turn_pair(modmul(freqs[:, :, None], places[None, None, :], modulus), modulus)
    curve = jnp.sin(math.pi * (places.astype(jnp.float32) + 0.5) / pixels)
    scaled = (0.25 + 0.75 * curve * curve) / math.sqrt(pixels)
    return ((jnp.stack([cosine, sine], axis=1) * scaled).astype(jnp.bfloat16), freqs)


def facet_turn(freqs, facet_ids, modulus, pixels, ratio):
    row_pos = facet_ids % ratio * pixels
    return turn_pair(modmul(freqs[:, :, None], row_pos[None, None, :], modulus), modulus)


def grid_table(size):
    places = jnp.arange(size, dtype=jnp.int32)
    angle = (places[:, None] * places[None, :] % size).astype(jnp.float32) * (two_pi / size)
    return (jnp.stack([jnp.cos(angle), jnp.sin(angle)]) / math.sqrt(size)).astype(jnp.bfloat16)


def slot_table(count, ratio):
    facet_ids = jnp.arange(count, dtype=jnp.int32)
    first = facet_ids % ratio
    second = facet_ids // ratio % ratio
    options = jnp.arange(ratio, dtype=jnp.int32)
    hits = (first[:, None, None] == options[None, :, None]) & (
        second[:, None, None] == options[None, None, :]
    )
    return hits.astype(jnp.bfloat16)


def finish_contrib(raw, turn_real, turn_imag):
    part_real = raw[:, 0, :, :, :, 0] - raw[:, 1, :, :, :, 1]
    part_imag = raw[:, 0, :, :, :, 1] + raw[:, 1, :, :, :, 0]
    real_turn = turn_real[:, :, :, None, None]
    imag_turn = turn_imag[:, :, :, None, None]
    out_real = real_turn * part_real - imag_turn * part_imag
    out_imag = real_turn * part_imag + imag_turn * part_real
    joined = jnp.stack([out_real, out_imag], axis=4)
    return jnp.transpose(joined, (0, 2, 3, 1, 4, 5)).astype(jnp.bfloat16)


def assemble(contrib, slots, grid):
    width = contrib.shape[2]
    terms = contrib.shape[1]
    ratio = slots.shape[1]
    size = width * ratio
    placed = jnp.einsum("fab,ftkcl->katclb", slots, contrib, preferred_element_type=jnp.float32)
    amatrix = placed.reshape(size, terms, 2, size).astype(jnp.bfloat16)
    first = jnp.einsum("zum,mtcn->zutcn", grid, amatrix, preferred_element_type=jnp.float32)
    front = jnp.stack(
        [first[0, :, :, 0] - first[1, :, :, 1], first[0, :, :, 1] + first[1, :, :, 0]], axis=2
    ).astype(jnp.bfloat16)
    second = jnp.einsum("utcn,zvn->utczv", front, grid, preferred_element_type=jnp.float32)
    sky_real = second[:, :, 0, 0] - second[:, :, 1, 1]
    sky_imag = second[:, :, 0, 1] + second[:, :, 1, 0]
    return jnp.stack([sky_real, sky_imag], axis=2).astype(jnp.bfloat16)


def degrid_grid(sky_grid, rows, count, observed):
    slots_count, channels, tile_height, span = observed.shape
    size = sky_grid.shape[0]
    nu_values = (jnp.arange(channels, dtype=jnp.float32) + 0.5) / channels - 0.5
    live = jnp.arange(slots_count, dtype=jnp.int32) < count
    target = rows[:, None] + jnp.arange(tile_height, dtype=jnp.int32)[None, :]
    hits = (target[:, :, None] == jnp.arange(size, dtype=jnp.int32)[None, None, :]) & live[
        :, None, None
    ]
    placer = hits.astype(jnp.bfloat16).reshape(slots_count * tile_height, size)
    model_rows = jnp.dot(
        placer, sky_grid.reshape(size, 2 * span), preferred_element_type=jnp.float32
    )
    model_rows = model_rows.reshape(slots_count, tile_height, 2, span)
    model = model_rows[:, None, :, 0] + nu_values[None, :, None, None] * model_rows[:, None, :, 1]
    residual = (observed.astype(jnp.float32) - model) * live[:, None, None, None].astype(
        jnp.float32
    )
    weighted = jnp.stack(
        [jnp.sum(residual, axis=1), jnp.sum(nu_values[None, :, None, None] * residual, axis=1)],
        axis=2,
    )
    weighted = weighted.astype(jnp.bfloat16).reshape(slots_count * tile_height, 2 * span)
    regrid = lax.dot_general(
        placer, weighted, (((0,), (0,)), ((), ())), preferred_element_type=jnp.float32
    )
    return (residual.astype(jnp.bfloat16), regrid.reshape(size, 2, 2, size).astype(jnp.bfloat16))


def adjoint_grid(regrid, grid):
    first = jnp.einsum("zum,utcv->zmtcv", grid, regrid, preferred_element_type=jnp.float32)
    back_real = first[0, :, :, 0] + first[1, :, :, 1]
    back_imag = first[0, :, :, 1] - first[1, :, :, 0]
    back_front = jnp.stack([back_real, back_imag], axis=2).astype(jnp.bfloat16)
    second = jnp.einsum("mtcv,zvn->mtczn", back_front, grid, preferred_element_type=jnp.float32)
    grid_real = second[:, :, 0, 0] + second[:, :, 1, 1]
    grid_imag = second[:, :, 1, 0] - second[:, :, 0, 1]
    return jnp.stack([grid_real, grid_imag], axis=2).astype(jnp.bfloat16)


def select_slots(back_grid, slots):
    ratio = slots.shape[1]
    size = back_grid.shape[0]
    width = size // ratio
    terms = back_grid.shape[1]
    shaped = back_grid.reshape(width, ratio, terms, 2, width, ratio)
    return jnp.einsum(
        "fab,katclb->ftkcl", slots, shaped, preferred_element_type=jnp.float32
    ).astype(jnp.bfloat16)


def turn_back(returned, turn_real, turn_imag):
    real_turn = jnp.transpose(turn_real, (0, 2, 1))[:, :, None, :, None]
    imag_turn = jnp.transpose(turn_imag, (0, 2, 1))[:, :, None, :, None]
    part_real = returned[:, :, :, :, 0].astype(jnp.float32)
    part_imag = returned[:, :, :, :, 1].astype(jnp.float32)
    turned = jnp.stack(
        [
            real_turn * part_real + imag_turn * part_imag,
            real_turn * part_imag - imag_turn * part_real,
        ],
        axis=4,
    )
    return turned.astype(jnp.bfloat16)


def paired_terms(turned):
    real_part = turned[:, :, :, :, 0]
    imag_part = turned[:, :, :, :, 1]
    pair_real = jnp.stack([real_part, imag_part], axis=1)
    pair_imag = jnp.stack([imag_part, -real_part], axis=1)
    return jnp.stack([pair_real, pair_imag], axis=5)


def strip_terms(table_part, paired):
    return jnp.einsum("szkp,szftkcl->pftcl", table_part, paired, preferred_element_type=jnp.float32)


def local(facet_model, sub_offsets, tile_rows, tile_counts, visibilities):
    facets_here = facet_model.shape[1]
    pixels = facet_model.shape[3]
    ratio = SG // CS
    pairs = lax.axis_size("sub")
    pair = lax.axis_index("sub")
    strip_group = lax.axis_index(("facet", "row"))
    facet_total = facets_here * pairs
    local_facets = pair * facets_here + jnp.arange(facets_here, dtype=jnp.int32)
    columns = column_table(local_facets, pixels, CS, SKY, ratio)
    strips = jnp.einsum(
        "tfpq,fckq->pftck", facet_model, columns, preferred_element_type=jnp.float32
    ).astype(jnp.bfloat16)
    group_offsets = lax.dynamic_slice_in_dim(sub_offsets, strip_group * pairs, pairs, 0)
    rtable, freqs = row_block(group_offsets, pixels, CS, SKY, pixels)
    turn_real, turn_imag = facet_turn(freqs, local_facets, SKY, pixels, ratio)
    table_part = rtable
    raw = jnp.einsum(
        "szkp,pftcl->szkftcl",
        table_part,
        lax.all_gather(strips, ("facet", "row"), axis=0, tiled=True),
        preferred_element_type=jnp.float32,
    )
    contrib = finish_contrib(raw, turn_real, turn_imag)
    slots = slot_table(facet_total, ratio)
    grid = grid_table(SG)
    sky_grid = assemble(
        lax.all_to_all(contrib, "sub", split_axis=0, concat_axis=1, tiled=True)[0], slots, grid
    )
    residual, regrid = degrid_grid(sky_grid, tile_rows[0], tile_counts[0], visibilities[0])
    back_grid = adjoint_grid(regrid, grid)
    returned = select_slots(back_grid, slots)[None]
    received = lax.all_to_all(returned, "sub", split_axis=1, concat_axis=0, tiled=True)
    turned = turn_back(received, turn_real, turn_imag)
    paired = paired_terms(turned)
    table_part = rtable
    mine = lax.psum_scatter(
        strip_terms(table_part, paired), ("facet", "row"), scatter_dimension=0, tiled=True
    )
    strip_round = mine.astype(jnp.bfloat16)
    residual_facets = jnp.einsum(
        "pftck,fckq->tfpq", strip_round, columns, preferred_element_type=jnp.float32
    ).astype(jnp.bfloat16)
    return (residual_facets, residual[None])


def solution(mesh):
    placed = (
        P(None, "sub", ("facet", "row"), None),
        P(),
        P(("facet", "row", "sub"), None),
        P(("facet", "row", "sub")),
        P(("facet", "row", "sub"), None, None, None, None),
    )
    return jax.shard_map(
        local,
        mesh=mesh,
        in_specs=placed,
        out_specs=(
            P(None, "sub", ("facet", "row"), None),
            P(("facet", "row", "sub"), None, None, None, None),
        ),
        check_vma=False,
    )
```

profile of v0, /device:TPU:2, one launch (start us, length us, event | category | flops | bytes accessed | tf_op | source)
XLA Modules:
  0.0 1020.6 jit_solution(10398024351297575194)
XLA Ops:
  7.8 19.9 %fusion.28 = (f32[2,1,64,8192]{3,2,1,0:T(8,128)S(1)}, f32[2,1,64,8192]{3,2,1,0:T(8,128)S(1)}) fusion(s32[2,8192]{1,0:T(2,128)S(1)} %get-tuple-element.37, s32[2,8192]{1,0:T(2,128)S(1)} %get-tuple-element.36, s32[64]{0:T(128)S(1)} %iota_multiply_fusion), kind=kLoop, calls=%fused_computation.58 | loop fusion | flops 40894464 | bytes 8519936 | tf_op jit(solution)/shard_map/cos | solution.py:27
  27.8 2.0 copy-done
  29.7 1.3 copy-done.1
  31.1 2.3 fusion.36
  35.9 21.4 %fusion.26 = (f32[2,1,64,8192]{3,2,1,0:T(8,128)}, f32[2,1,64,8192]{3,2,1,0:T(8,128)}) fusion(s32[8192]{0:T(1024)S(1)} %get-tuple-element.44, s32[8192]{0:T(1024)S(1)} %get-tuple-element.45, s32[2,64]{1,0:T(2,128)S(1)} %and_select_fusion.15), kind=kLoop, calls=%fused_computation.56 | loop fusion | flops 40894464 | bytes 8454656 | tf_op jit(solution)/shard_map/cos | solution.py:27
  57.3 130.4 %all-gather.2.cloned.1.call-done = bf16[8192,2,2,2,64]{4,3,2,1,0:T(2,128)(2,1)} async-done(((bf16[64,2,2,2,64]{4,3,2,1,0:T(2,128)(2,1)}), bf16[8192,2,2,2,64]{4,3,2,1,0:T(2,128)(2,1)}) %all-gather.2.cloned.1.call-update) | async-done | bytes 8388624 | tf_op jit(solution)/shard_map/all_gather | solution.py:198
  187.7 10.6 %fusion = f32[2,2,64,2,2,2,64]{6,2,5,4,3,1,0:T(8,128)S(1)} fusion(bf16[8192,2,2,2,64,1,1]{4,3,2,1,0,6,5:T(2,128)(2,1)} %bitcast.270, f32[2,1,64,8192]{3,2,1,0:T(8,128)} %get-tuple-element.29, f32[2,1,64,8192]{3,2,1,0:T(8,128)} %get-tuple-element.28, f32[8192]{0:T(1024)S(1)} %fusion.101), kind=kOutput, calls=%fused_computation.1 | convolution fusion | flops 2153775104 | bytes 17334272 | tf_op jit(solution)/shard_map/szkp,pftcl->szkftcl/dot_general | solution.py:195
  198.5 0.9 reshape.1156
  199.4 4.8 all-to-all-start
  204.2 2.7 all-to-all-done
  207.9 6.6 copy.128
  214.4 13.1 %reshape.1144 = bf16[128,2,2,128,1]{3,0,2,1,4:T(8,128)(2,1)S(1)} reshape(bf16[64,2,2,2,64,2]{5,4,1,0,3,2:T(8,128)(2,1)} %copy.128) | data formatting | bytes 262144 | tf_op jit(solution)/shard_map/convert_element_type | solution.py:89
  229.6 10.0 add.648
  239.6 3.9 copy.141
  243.5 10.0 sub.140
  253.5 3.9 copy.142
  258.1 0.9 reshape.1158
  259.0 5.1 all-to-all-start.1
  264.2 2.3 all-to-all-done.1
  267.2 16.6 %convolution_bitcast_fusion = f32[8192,2,2,2,64]{4,0,3,2,1:T(8,128)} fusion(bf16[2,2,2,2,64,1,64]{6,4,1,0,5,3,2:T(8,128)(2,1)S(1)} %get-tuple-element.27, bf16[2,2,2,2,64,1,64]{6,4,1,0,5,3,2:T(8,128)(2,1)S(1)} %get-tuple-element.26, f32[2,1,64,8192]{3,2,1,0:T(8,128)} %get-tuple-element.29, f32[2,1,64,8192]{3,2,1,0:T(8,128)} %get-tuple-element.28, ...), kind=kOutput, calls=%fused_computation | convolution fusion | flops 2154299392 | bytes 25460736 | tf_op jit(solution)/shard_map/szkp,szftkcl->pftcl/dot_general | solution.py:175
  283.9 1.2 fusion.42
  285.1 721.6 %reduce-scatter.2.cloned.1.call-done = f32[64,2,2,2,64]{4,0,3,2,1:T(8,128)} async-done(((f32[8192,2,2,2,64]{4,0,3,2,1:T(8,128)}), f32[64,2,2,2,64]{4,0,3,2,1:T(8,128)}) %reduce-scatter.2.cloned.1.call-update) | async-done | bytes 131088 | tf_op jit(solution)/shard_map/reduce_scatter | solution.py:214
  1006.7 4.8 fusion.3
  1011.5 2.3 copy.148
  (70 shorter events, 7.0 us)
Async XLA Ops:
  7.2 180.5 %all-gather.2.cloned.1.call-start = ((), (), s32[]{:S(2)}) async-start(), calls=%async_computation.3 | async-start | bytes 16908288 | tf_op jit(solution)/shard_map/all_gather | solution.py:198
  7.8 23.3 %copy-start.4 = (bf16[2,2,64,8192]{3,2,1,0:T(8,128)(2,1)S(1)}, bf16[2,2,64,8192]{3,2,1,0:T(8,128)(2,1)}, u32[]{:S(2)}) copy-start(bf16[2,2,64,8192]{3,2,1,0:T(8,128)(2,1)} %param.5) | copy-start | bytes 12582916
  27.7 2.0 copy-start
  27.8 3.3 copy-start.1
  31.1 3.9 copy-start.3
  31.1 4.1 copy-start.5
  199.4 7.5 all-to-all-start
  214.4 13.9 %copy-start.2 = (bf16[1,4,32,8,256]{4,3,2,1,0:T(8,128)(2,1)S(1)}, bf16[1,4,32,8,256]{4,3,2,1,0:T(8,128)(2,1)}, u32[]{:S(2)}) copy-start(bf16[1,4,32,8,256]{4,3,2,1,0:T(8,128)(2,1)} %param.9) | copy-start | bytes 1572868
  259.0 7.6 all-to-all-start.1
  264.1 742.6 %reduce-scatter.2.cloned.1.call-start = ((), (), s32[]{:S(2)}) async-start(), calls=%async_computation.4 | async-start | bytes 33816576 | tf_op jit(solution)/shard_map/reduce_scatter | solution.py:214
Sparse Core Ops, SparseCore 0:
  34.3 153.3 all-gather.1
  284.0 722.6 reduce-scatter.1
where the time goes:
time: 1020 us
  waiting for transfers between devices  857 us (84%)
  local copies, waits for them, and re-layouts  57 us (6%)
  other arithmetic  45 us (4%)
  matrix products  36.5 us (4%)
  between operations  15.1 us (1%)
    reduce_scatter x1, waiting for transfers between devices, local(): lax.psum_scatter(strip_terms(table_part, paired), ('facet', 'row'), scatt...  722 us
    all_gather x1, waiting for transfers between devices, local(): lax.all_gather(strips, ('facet', 'row'), axis=0, tiled=True)  130 us
    cos x4, other arithmetic, turn_pair(): return (jnp.cos(angle), jnp.sin(angle))  41.6 us
  transfers between devices with their start and end apart: 4, of which 4 were waited for; matrix products, arithmetic and copies ran while one was open for 2% of the time, Pallas kernels for 0%

commit v1 on v0

--- a/solution.py
+++ b/solution.py
@@ -3,6 +3,7 @@
 import jax.numpy as jnp
 from jax import lax
 from jax.sharding import PartitionSpec as P
+from jax.lax import all_to_all, axis_size
 
 SKY = 65536
 CS = 64
@@ -192,11 +193,14 @@
     rtable, freqs = row_block(group_offsets, pixels, CS, SKY, pixels)
     turn_real, turn_imag = facet_turn(freqs, local_facets, SKY, pixels, ratio)
     table_part = rtable
+
+    def slots_get(values):
+        e_now = jnp.stack([values for _ in range(axis_size(("facet", "row")))])
+        s_next = all_to_all(e_now, ("facet", "row"), split_axis=0, concat_axis=0)
+        return jnp.concatenate(s_next, axis=0)
+
     raw = jnp.einsum(
-        "szkp,pftcl->szkftcl",
-        table_part,
-        lax.all_gather(strips, ("facet", "row"), axis=0, tiled=True),
-        preferred_element_type=jnp.float32,
+        "szkp,pftcl->szkftcl", table_part, slots_get(strips), preferred_element_type=jnp.float32
     )
     contrib = finish_contrib(raw, turn_real, turn_imag)
     slots = slot_table(facet_total, ratio)

time: 1020 us -> 1180 us (1.16)
  local copies, waits for them, and re-layouts: 57 us -> 166 us
  waiting for transfers between devices: 857 us -> 886 us
  starting transfers between devices: 9.98 us -> 25.8 us
    all_to_all x0 -> x1, waiting for transfers between devices: none -> 165 us  [slots_get(): s_next = all_to_all(e_now, ('facet', 'row'), split_axis=0, concat_axis=0)]
    all_gather x1 -> x0, waiting for transfers between devices: 130 us -> none  [local(): lax.all_gather(strips, ('facet', 'row'), axis=0, tiled=True)]
    unnamed x18 -> x21, local copies, waits for them, and re-layouts: 7.85 us -> 76.5 us
    reshape x0 -> x1, local copies, waits for them, and re-layouts: none -> 22.5 us  [slots_get(): return jnp.concatenate(s_next, axis=0)]
    all_to_all x0 -> x1, local copies, waits for them, and re-layouts: none -> 18.6 us  [slots_get(): s_next = all_to_all(e_now, ('facet', 'row'), split_axis=0, concat_axis=0)]
    all_to_all x0 -> x1, starting transfers between devices: none -> 15.6 us  [slots_get(): s_next = all_to_all(e_now, ('facet', 'row'), split_axis=0, concat_axis=0)]
where the time goes in v1:
time: 1180 us; the launch traced here: 1170 us
  waiting for transfers between devices  886 us (75%)
  local copies, waits for them, and re-layouts  166 us (14%)
  other arithmetic  44.8 us (4%)
  matrix products  34.1 us (3%)
  starting transfers between devices  25.8 us (2%)
  between operations  15.5 us (1%)
    reduce_scatter x1, waiting for transfers between devices, local(): lax.psum_scatter(strip_terms(table_part, paired), ('facet', 'row'), scatt...  716 us
    all_to_all x1, waiting for transfers between devices, slots_get(): s_next = all_to_all(e_now, ('facet', 'row'), split_axis=0, concat_axis=0)  165 us
    unnamed x21, local copies, waits for them, and re-layouts  76.5 us
    cos x4, other arithmetic, turn_pair(): return (jnp.cos(angle), jnp.sin(angle))  41.4 us
  transfers between devices with their start and end apart: 4, of which 4 were waited for; matrix products, arithmetic and copies ran while one was open for 2% of the time, Pallas kernels for 0%

profile of v1, /device:TPU:2, one launch (start us, length us, event | category | flops | bytes accessed | tf_op | source)
XLA Modules:
  0.0 1172.2 jit_solution(4635313772098552250)
XLA Ops:
  7.8 19.7 %fusion.29 = (f32[2,1,64,8192]{3,2,1,0:T(8,128)S(1)}, f32[2,1,64,8192]{3,2,1,0:T(8,128)S(1)}) fusion(s32[2,8192]{1,0:T(2,128)S(1)} %get-tuple-element.37, s32[2,8192]{1,0:T(2,128)S(1)} %get-tuple-element.36, s32[64]{0:T(128)S(1)} %iota_multiply_fusion), kind=kLoop, calls=%fused_computation.59 | loop fusion | flops 40894464 | bytes 8519936 | tf_op jit(solution)/shard_map/cos | solution.py:28
  30.8 16.2 %broadcast_bitcast_fusion = bf16[128,2,2,2,64,64]{5,4,3,2,1,0:T(8,128)(2,1)} fusion(bf16[64,2,2,2,64]{0,4,2,3,1:T(8,128)(2,1)S(1)} %fusion.39), kind=kLoop, calls=%fused_computation.297 | loop fusion | bytes 8454144
  47.1 27.1 %reshape.1163 = bf16[128,2,16384]{2,1,0:T(2,128)(2,1)} reshape(bf16[128,2,2,2,64,64]{5,4,3,2,1,0:T(8,128)(2,1)} %broadcast_bitcast_fusion) | data formatting | bytes 16777216
  74.2 15.6 %all-to-all-start = ((bf16[128,2,16384]{2,1,0:T(2,128)(2,1)}), bf16[128,2,16384]{2,1,0:T(2,128)(2,1)}, u32[]{:S(2)}, u32[]{:S(2)}) async-start(bf16[128,2,16384]{2,1,0:T(2,128)(2,1)} %reshape.1163), calls=%async_computation | async-start | bytes 16777216 | tf_op jit(solution)/shard_map/all_to_all | solution.py:199
  91.5 21.4 %fusion.27 = (f32[2,1,64,8192]{3,2,1,0:T(8,128)}, f32[2,1,64,8192]{3,2,1,0:T(8,128)}) fusion(s32[8192]{0:T(1024)S(1)} %get-tuple-element.44, s32[8192]{0:T(1024)S(1)} %get-tuple-element.45, s32[2,64]{1,0:T(2,128)S(1)} %and_select_fusion.15), kind=kLoop, calls=%fused_computation.57 | loop fusion | flops 40894464 | bytes 8454656 | tf_op jit(solution)/shard_map/cos | solution.py:28
  112.9 165.2 %all-to-all-done = bf16[128,2,16384]{2,1,0:T(2,128)(2,1)} async-done(((bf16[128,2,16384]{2,1,0:T(2,128)(2,1)}), bf16[128,2,16384]{2,1,0:T(2,128)(2,1)}, u32[]{:S(2)}, u32[]{:S(2)}) %all-to-all-start) | async-done | bytes 8388640 | tf_op jit(solution)/shard_map/all_to_all | solution.py:199
  278.1 27.6 %reshape.1164 = bf16[128,2,2,2,64,64]{5,4,3,2,1,0:T(8,128)(2,1)} reshape(bf16[128,2,16384]{2,1,0:T(2,128)(2,1)} %all-to-all-done) | data formatting | bytes 16777216
  305.7 18.6 %copy.127 = bf16[128,64,2,2,2,64]{1,0,5,4,3,2:T(8,128)(2,1)} copy(bf16[128,64,2,2,2,64]{1,5,4,3,2,0:T(8,128)(2,1)} %bitcast.276) | data formatting | bytes 16777216 | tf_op jit(solution)/shard_map/all_to_all | solution.py:199
  324.3 22.5 %reshape.1146 = bf16[8192,2,2,2,64,1,1]{0,4,3,2,1,5,6:T(8,128)(2,1)} reshape(bf16[128,64,2,2,2,64]{1,0,5,4,3,2:T(8,128)(2,1)} %copy.127) | data formatting | bytes 16777216 | tf_op jit(solution)/shard_map/reshape | solution.py:200
  346.9 8.2 fusion.4
  356.3 4.8 all-to-all-start.1
  361.1 2.5 all-to-all-done.1
  364.5 6.6 copy.132
  371.0 13.1 %reshape.1150 = bf16[128,2,2,128,1]{3,0,2,1,4:T(8,128)(2,1)S(1)} reshape(bf16[64,2,2,2,64,2]{5,4,1,0,3,2:T(8,128)(2,1)} %copy.132) | data formatting | bytes 262144 | tf_op jit(solution)/shard_map/convert_element_type | solution.py:90
  386.2 10.0 sub.140
  396.2 3.9 copy.146
  400.1 10.0 add.648
  410.1 3.9 copy.145
  415.6 5.4 all-to-all-start.2
  421.1 2.3 all-to-all-done.2
  424.1 16.6 %convolution_bitcast_fusion = f32[8192,2,2,2,64]{4,0,3,2,1:T(8,128)} fusion(bf16[2,2,2,2,64,1,64]{6,4,1,0,5,3,2:T(8,128)(2,1)S(1)} %get-tuple-element.27, bf16[2,2,2,2,64,1,64]{6,4,1,0,5,3,2:T(8,128)(2,1)S(1)} %get-tuple-element.26, f32[2,1,64,8192]{3,2,1,0:T(8,128)} %get-tuple-element.29, f32[2,1,64,8192]{3,2,1,0:T(8,128)} %get-tuple-element.28, ...), kind=kOutput, calls=%fused_computation | convolution fusion | flops 2154299392 | bytes 25460736 | tf_op jit(solution)/shard_map/szkp,szftkcl->pftcl/dot_general | solution.py:176
  441.9 716.0 %reduce-scatter.2.cloned.1.call-done = f32[64,2,2,2,64]{4,0,3,2,1:T(8,128)} async-done(((f32[8192,2,2,2,64]{4,0,3,2,1:T(8,128)}), f32[64,2,2,2,64]{4,0,3,2,1:T(8,128)}) %reduce-scatter.2.cloned.1.call-update) | async-done | bytes 131088 | tf_op jit(solution)/shard_map/reduce_scatter | solution.py:218
  1157.9 4.8 fusion.1
  1162.7 2.3 copy.152
  (73 shorter events, 12.4 us)
Async XLA Ops:
  7.8 19.8 %copy-start.4 = (bf16[2,2,64,8192]{3,2,1,0:T(8,128)(2,1)S(1)}, bf16[2,2,64,8192]{3,2,1,0:T(8,128)(2,1)}, u32[]{:S(2)}) copy-start(bf16[2,2,64,8192]{3,2,1,0:T(8,128)(2,1)} %param.5) | copy-start | bytes 12582916
  27.5 2.3 copy-start
  27.5 3.3 copy-start.1
  74.2 16.2 %copy-start.3 = (s32[1,4]{1,0:T(1,128)S(1)}, s32[1,4]{1,0:T(1,128)}, u32[]{:S(2)}) copy-start(s32[1,4]{1,0:T(1,128)} %param.7) | copy-start | bytes 52
  74.2 16.6 %copy-start.5 = (s32[256]{0:T(256)S(1)}, s32[256]{0:T(256)}, u32[]{:S(2)}) copy-start(s32[256]{0:T(256)} %param.6) | copy-start | bytes 3076
  74.2 203.9 %all-to-all-start = ((bf16[128,2,16384]{2,1,0:T(2,128)(2,1)}), bf16[128,2,16384]{2,1,0:T(2,128)(2,1)}, u32[]{:S(2)}, u32[]{:S(2)}) async-start(bf16[128,2,16384]{2,1,0:T(2,128)(2,1)} %reshape.1163), calls=%async_computation | async-start | bytes 16777216 | tf_op jit(solution)/shard_map/all_to_all | solution.py:199
  356.3 7.3 all-to-all-start.1
  371.0 13.9 %copy-start.2 = (bf16[1,4,32,8,256]{4,3,2,1,0:T(8,128)(2,1)S(1)}, bf16[1,4,32,8,256]{4,3,2,1,0:T(8,128)(2,1)}, u32[]{:S(2)}) copy-start(bf16[1,4,32,8,256]{4,3,2,1,0:T(8,128)(2,1)} %param.9) | copy-start | bytes 1572868
  415.6 7.8 all-to-all-start.2
  421.0 736.9 %reduce-scatter.2.cloned.1.call-start = ((), (), s32[]{:S(2)}) async-start(), calls=%async_computation.4 | async-start | bytes 33816576 | tf_op jit(solution)/shard_map/reduce_scatter | solution.py:218
Sparse Core Ops, SparseCore 0:
  440.9 716.9 reduce-scatter.1
